TPU v7x, 128 devices: a whole 4x4x4 slice. The times are simulated.
128 devices in a mesh: dp: 16 (over z, x), seq: 8 (over y, core).
Axes of the slice: x: 4, y: 4, z: 4, core: 2. Of those that a mesh axis runs over, the one named last changes fastest.
Arguments:
- layer_input: bfloat16 [2, 16, 1024, 896], P(None, 'dp', 'seq'), may hold values from -6 to 6
- pic_start: int32 [2, 16], P(None, 'dp'), may hold values from 0 to 768, as said below
- norm_one: bfloat16 [896], P('dp'), may hold values from 0.099609375 to 1.8984375
- w_query: bfloat16 [896, 896], P('dp'), may hold values from -0.1875 to 0.1875
- b_query: bfloat16 [896], P('dp'), may hold values from -3 to 3
- w_key: bfloat16 [896, 128], P('dp'), may hold values from -0.1875 to 0.1875
- b_key: bfloat16 [128], P('dp'), may hold values from -3 to 3
- w_value: bfloat16 [896, 128], P('dp'), may hold values from -0.1875 to 0.1875
- b_value: bfloat16 [128], P('dp'), may hold values from -3 to 3
- w_out: bfloat16 [896, 896], P('dp'), may hold values from -1.5 to 1.5
- norm_two: bfloat16 [896], P('dp'), may hold values from 0.099609375 to 1.8984375
- w_gate: bfloat16 [896, 4864], P('dp'), may hold values from -0.1875 to 0.1875
- w_up: bfloat16 [896, 4864], P('dp'), may hold values from -0.1875 to 0.1875
- w_down: bfloat16 [4864, 896], P('dp'), may hold values from -0.078125 to 0.078125
- out_grad: bfloat16 [2, 16, 1024, 896], P(None, 'dp', 'seq'), may hold values from -6 to 6
Outputs:
- layer_output: bfloat16 [2, 16, 1024, 896], P(None, 'dp', 'seq')
- input_grad: float32 [2, 16, 1024, 896], P(None, 'dp', 'seq')
- norm_one_grad: float32 [896], P('dp')
- w_query_grad: float32 [896, 896], P('dp')
- b_query_grad: float32 [896], P('dp')
- w_key_grad: float32 [896, 128], P('dp')
- b_key_grad: float32 [128], P('dp')
- w_value_grad: float32 [896, 128], P('dp')
- b_value_grad: float32 [128], P('dp')
- w_out_grad: float32 [896, 896], P('dp')
- norm_two_grad: float32 [896], P('dp')
- w_gate_grad: float32 [896, 4864], P('dp')
- w_up_grad: float32 [896, 4864], P('dp')
- w_down_grad: float32 [4864, 896], P('dp')
Inputs may be any that keep to these rules, and one draw needn't show every extreme that they name: Each sequence has one picture block of 256 tokens starting at its pic_start, a multiple of 256.
All inputs are finite; a program needn't handle non-finite values.
Results may differ from a plain program's by a relative error of at most 0.028.
Values may be sent and summed in bfloat16 or wider, within the bound.
A program may use at most 192 MiB of HBM per device.

v0:
```python
import jax
import jax.numpy as jnp
from jax import lax
from jax.sharding import PartitionSpec as P

HEADS = 14
KV_HEADS = 2
HD = 64
PIC = 256
EPSILON = 1e-06
ROPE_BASE = 1000000.0
NEGATIVE = -1e30


def rope_tables(positions, head_dim):
    half_dim = head_dim // 2
    exponent = jnp.arange(half_dim, dtype=jnp.float32) * (2.0 / head_dim)
    inverse = ROPE_BASE ** (-exponent)
    angles = positions.astype(jnp.float32)[:, None] * inverse[None, :]
    angles = jnp.concatenate([angles, angles], axis=1)
    return (jnp.cos(angles), jnp.sin(angles))


def rotate_half(inputs, head_dim):
    shaped = inputs.reshape(inputs.shape[:-1] + (inputs.shape[-1] // head_dim, 2, head_dim // 2))
    turned = jnp.stack([-shaped[..., 1, :], shaped[..., 0, :]], axis=-2)
    return turned.reshape(inputs.shape)


def rotate(inputs, cosine, sine, head_dim, direction):
    count = inputs.shape[-1] // head_dim
    cos_all = jnp.tile(cosine, (1, count))
    sin_all = jnp.tile(sine, (1, count))
    return inputs * cos_all + direction * rotate_half(inputs, head_dim) * sin_all


def visible_mask(query_pos, key_pos, start):
    inside_query = (query_pos >= start) & (query_pos < start + PIC)
    inside_key = (key_pos >= start) & (key_pos < start + PIC)
    return (key_pos[None, :] <= query_pos[:, None]) | inside_query[:, None] & inside_key[None, :]


def norm_rows(inputs, gain_row):
    inverse = lax.rsqrt(jnp.mean(inputs * inputs, axis=-1, keepdims=True) + EPSILON)
    return (inverse, inputs * inverse * gain_row)


def norm_back(inputs, inverse, gain_row, grad_normed):
    scaled_in = inputs * inverse
    gain_grad = jnp.sum(grad_normed * scaled_in, axis=0)
    weighted = grad_normed * gain_row
    grad_in = inverse * weighted - scaled_in * inverse * jnp.mean(
        weighted * scaled_in, axis=-1, keepdims=True
    )
    return (grad_in, gain_grad)


def outer_sum(left, right):
    return jnp.einsum("ta,tb->ab", left, right, preferred_element_type=jnp.float32)


def back_dot(grad_rows, weight):
    return jnp.einsum("tb,ab->ta", grad_rows, weight, preferred_element_type=jnp.float32)


def per_device(
    layer_input,
    pic_start,
    norm_one,
    w_query,
    b_query,
    w_key,
    b_key,
    w_value,
    b_value,
    w_out,
    norm_two,
    w_gate,
    w_up,
    w_down,
    out_grad,
):
    micro_count, seq_count, row_count, model_width = layer_input.shape
    length = row_count * lax.axis_size("seq")
    tokens = seq_count * row_count
    group = HEADS // KV_HEADS
    score_scale = HD ** (-0.5)
    query_pos = lax.axis_index("seq") * row_count + jnp.arange(row_count, dtype=jnp.int32)
    key_pos = jnp.arange(length, dtype=jnp.int32)
    cosine, sine = rope_tables(jnp.tile(query_pos, seq_count), HD)

    def scores_of(query_heads, key_heads, start):
        scores = (
            jnp.einsum("rkgd,lkd->kgrl", query_heads, key_heads, preferred_element_type=jnp.float32)
            * score_scale
        )
        return jnp.where(visible_mask(query_pos, key_pos, start), scores, NEGATIVE)

    def attend_forward(element):
        q_seq, k_seq, v_seq, start = element
        query_heads = q_seq.reshape(row_count, KV_HEADS, group, HD)
        key_heads = k_seq.reshape(length, KV_HEADS, HD)
        value_heads = v_seq.reshape(length, KV_HEADS, HD)
        masked = scores_of(query_heads, key_heads, start)
        row_max = jnp.max(masked, axis=-1, keepdims=True)
        unnormed = jnp.exp(masked - row_max)
        row_total = jnp.sum(unnormed, axis=-1, keepdims=True)
        probs = (unnormed / row_total).astype(jnp.bfloat16)
        attended = jnp.einsum(
            "kgrl,lkd->rkgd", probs, value_heads, preferred_element_type=jnp.float32
        )
        return (
            attended.reshape(row_count, HEADS * HD).astype(jnp.bfloat16),
            row_max + jnp.log(row_total),
        )

    def attend_backward(element):
        q_seq, k_seq, v_seq, start, log_total, grad_seq = element
        query_heads = q_seq.reshape(row_count, KV_HEADS, group, HD)
        key_heads = k_seq.reshape(length, KV_HEADS, HD)
        value_heads = v_seq.reshape(length, KV_HEADS, HD)
        grad_heads = grad_seq.reshape(row_count, KV_HEADS, group, HD)
        probs = jnp.exp(scores_of(query_heads, key_heads, start) - log_total)
        rounded = probs.astype(jnp.bfloat16)
        prob_grad = jnp.einsum(
            "rkgd,lkd->kgrl", grad_heads, value_heads, preferred_element_type=jnp.float32
        )
        centre = jnp.sum(probs * prob_grad, axis=-1, keepdims=True)
        score_grad = (probs * (prob_grad - centre)).astype(jnp.bfloat16)
        query_grad = (
            jnp.einsum("kgrl,lkd->rkgd", score_grad, key_heads, preferred_element_type=jnp.float32)
            * score_scale
        )
        key_grad = (
            jnp.einsum(
                "kgrl,rkgd->lkd", score_grad, query_heads, preferred_element_type=jnp.float32
            )
            * score_scale
        )
        value_grad = jnp.einsum(
            "kgrl,rkgd->lkd", rounded, grad_heads, preferred_element_type=jnp.float32
        )
        return (
            query_grad.reshape(row_count, HEADS * HD),
            key_grad.reshape(length, KV_HEADS * HD),
            value_grad.reshape(length, KV_HEADS * HD),
        )

    totals = None
    outputs = []
    input_grads = []
    for micro_index in range(micro_count):
        attn_full = (
            lax.all_gather(norm_one, "dp", axis=0, tiled=True),
            lax.all_gather(w_query, "dp", axis=0, tiled=True),
            lax.all_gather(b_query, "dp", axis=0, tiled=True),
            lax.all_gather(w_key, "dp", axis=0, tiled=True),
            lax.all_gather(b_key, "dp", axis=0, tiled=True),
            lax.all_gather(w_value, "dp", axis=0, tiled=True),
            lax.all_gather(b_value, "dp", axis=0, tiled=True),
            lax.all_gather(w_out, "dp", axis=0, tiled=True),
        )
        mlp_full = (
            lax.all_gather(norm_two, "dp", axis=0, tiled=True),
            lax.all_gather(w_gate, "dp", axis=0, tiled=True),
            lax.all_gather(w_up, "dp", axis=0, tiled=True),
            lax.all_gather(w_down, "dp", axis=0, tiled=True),
        )
        gain_one, query_full, qbias_full, key_full, kbias_full, value_full, vbias_full, out_full = (
            attn_full
        )
        inputs = layer_input[micro_index].reshape(tokens, model_width).astype(jnp.float32)
        inv_one, normed_float = norm_rows(inputs, gain_one.astype(jnp.float32))
        normed = normed_float.astype(jnp.bfloat16)
        query_lin = jnp.dot(
            normed, query_full, preferred_element_type=jnp.float32
        ) + qbias_full.astype(jnp.float32)
        key_lin = jnp.dot(normed, key_full, preferred_element_type=jnp.float32) + kbias_full.astype(
            jnp.float32
        )
        value_lin = jnp.dot(
            normed, value_full, preferred_element_type=jnp.float32
        ) + vbias_full.astype(jnp.float32)
        queries = rotate(query_lin, cosine, sine, HD, 1.0).astype(jnp.bfloat16)
        keys = rotate(key_lin, cosine, sine, HD, 1.0).astype(jnp.bfloat16)
        values = value_lin.astype(jnp.bfloat16)
        keys_all, values_all = (
            lax.all_gather(
                keys.reshape(seq_count, row_count, KV_HEADS * HD), "seq", axis=1, tiled=True
            ),
            lax.all_gather(
                values.reshape(seq_count, row_count, KV_HEADS * HD), "seq", axis=1, tiled=True
            ),
        )
        query_seqs = queries.reshape(seq_count, row_count, HEADS * HD)
        starts = pic_start[micro_index]
        attended, log_total = lax.map(attend_forward, (query_seqs, keys_all, values_all, starts))
        att_rows = attended.reshape(tokens, HEADS * HD)
        resid = inputs + jnp.dot(att_rows, out_full, preferred_element_type=jnp.float32)
        gain_two, gate_full, up_full, down_full = mlp_full
        inv_two, normed_two_float = norm_rows(resid, gain_two.astype(jnp.float32))
        normed_two = normed_two_float.astype(jnp.bfloat16)
        gate_float = lax.optimization_barrier(
            jnp.dot(normed_two, gate_full, preferred_element_type=jnp.float32).astype(jnp.bfloat16)
        ).astype(jnp.float32)
        up_float = lax.optimization_barrier(
            jnp.dot(normed_two, up_full, preferred_element_type=jnp.float32).astype(jnp.bfloat16)
        ).astype(jnp.float32)
        sigmoid_gate = jax.nn.sigmoid(gate_float)
        hidden = (gate_float * sigmoid_gate * up_float).astype(jnp.bfloat16)
        output = resid + jnp.dot(hidden, down_full, preferred_element_type=jnp.float32)
        outputs.append(output.astype(jnp.bfloat16).reshape(seq_count, row_count, model_width))
        attn_back = (
            lax.all_gather(norm_one, "dp", axis=0, tiled=True),
            lax.all_gather(w_query, "dp", axis=0, tiled=True),
            lax.all_gather(b_query, "dp", axis=0, tiled=True),
            lax.all_gather(w_key, "dp", axis=0, tiled=True),
            lax.all_gather(b_key, "dp", axis=0, tiled=True),
            lax.all_gather(w_value, "dp", axis=0, tiled=True),
            lax.all_gather(b_value, "dp", axis=0, tiled=True),
            lax.all_gather(w_out, "dp", axis=0, tiled=True),
        )
        mlp_back = (
            lax.all_gather(norm_two, "dp", axis=0, tiled=True),
            lax.all_gather(w_gate, "dp", axis=0, tiled=True),
            lax.all_gather(w_up, "dp", axis=0, tiled=True),
            lax.all_gather(w_down, "dp", axis=0, tiled=True),
        )
        (
            gain_one_back,
            query_back,
            qbias_back,
            key_back,
            kbias_back,
            value_back,
            vbias_back,
            out_back,
        ) = attn_back
        gain_two_back, gate_back, up_back, down_back = mlp_back
        grad_rows = out_grad[micro_index].reshape(tokens, model_width)
        down_grad = outer_sum(hidden, grad_rows)
        hidden_grad = lax.optimization_barrier(
            back_dot(grad_rows, down_back).astype(jnp.bfloat16)
        ).astype(jnp.float32)
        gate_grad_low = (
            hidden_grad * up_float * sigmoid_gate * (1.0 + gate_float * (1.0 - sigmoid_gate))
        ).astype(jnp.bfloat16)
        up_grad_low = (hidden_grad * gate_float * sigmoid_gate).astype(jnp.bfloat16)
        gate_wgrad = outer_sum(normed_two, gate_grad_low)
        up_wgrad = outer_sum(normed_two, up_grad_low)
        grad_normed_two = back_dot(gate_grad_low, gate_back) + back_dot(up_grad_low, up_back)
        grad_middle, gain_two_grad = norm_back(
            resid, inv_two, gain_two_back.astype(jnp.float32), grad_normed_two
        )
        resid_grad = grad_rows.astype(jnp.float32) + grad_middle
        attn_grad_low = resid_grad.astype(jnp.bfloat16)
        out_wgrad = outer_sum(att_rows, attn_grad_low)
        heads_grad = back_dot(attn_grad_low, out_back).astype(jnp.bfloat16)
        query_grad, key_part, value_part = lax.map(
            attend_backward,
            (
                query_seqs,
                keys_all,
                values_all,
                starts,
                log_total,
                heads_grad.reshape(seq_count, row_count, HEADS * HD),
            ),
        )
        key_grad, value_grad = (
            lax.psum_scatter(
                key_part.astype(jnp.bfloat16), "seq", scatter_dimension=1, tiled=True
            ).astype(jnp.float32),
            lax.psum_scatter(
                value_part.astype(jnp.bfloat16), "seq", scatter_dimension=1, tiled=True
            ).astype(jnp.float32),
        )
        qlin_grad = rotate(query_grad.reshape(tokens, HEADS * HD), cosine, sine, HD, -1.0).astype(
            jnp.bfloat16
        )
        klin_grad = rotate(key_grad.reshape(tokens, KV_HEADS * HD), cosine, sine, HD, -1.0).astype(
            jnp.bfloat16
        )
        vlin_grad = value_grad.reshape(tokens, KV_HEADS * HD).astype(jnp.bfloat16)
        grad_normed = (
            back_dot(qlin_grad, query_back)
            + back_dot(klin_grad, key_back)
            + back_dot(vlin_grad, value_back)
        )
        grad_first, gain_one_grad = norm_back(
            inputs, inv_one, gain_one_back.astype(jnp.float32), grad_normed
        )
        input_grads.append((resid_grad + grad_first).reshape(seq_count, row_count, model_width))
        batch_grads = (
            gain_one_grad,
            outer_sum(normed, qlin_grad),
            jnp.sum(qlin_grad.astype(jnp.float32), axis=0),
            outer_sum(normed, klin_grad),
            jnp.sum(klin_grad.astype(jnp.float32), axis=0),
            outer_sum(normed, vlin_grad),
            jnp.sum(vlin_grad.astype(jnp.float32), axis=0),
            out_wgrad,
            gain_two_grad,
            gate_wgrad,
            up_wgrad,
            down_grad,
        )
        totals = batch_grads if totals is None else jax.tree.map(jnp.add, totals, batch_grads)
    shares = (
        lax.psum_scatter(totals[0], "dp", scatter_dimension=0, tiled=True),
        lax.psum_scatter(totals[1], "dp", scatter_dimension=0, tiled=True),
        lax.psum_scatter(totals[2], "dp", scatter_dimension=0, tiled=True),
        lax.psum_scatter(totals[3], "dp", scatter_dimension=0, tiled=True),
        lax.psum_scatter(totals[4], "dp", scatter_dimension=0, tiled=True),
        lax.psum_scatter(totals[5], "dp", scatter_dimension=0, tiled=True),
        lax.psum_scatter(totals[6], "dp", scatter_dimension=0, tiled=True),
        lax.psum_scatter(totals[7], "dp", scatter_dimension=0, tiled=True),
        lax.psum_scatter(totals[8], "dp", scatter_dimension=0, tiled=True),
        lax.psum_scatter(totals[9], "dp", scatter_dimension=0, tiled=True),
        lax.psum_scatter(totals[10], "dp", scatter_dimension=0, tiled=True),
        lax.psum_scatter(totals[11], "dp", scatter_dimension=0, tiled=True),
    )
    shares = (
        lax.psum(shares[0].astype(jnp.bfloat16), "seq").astype(jnp.float32),
        lax.psum(shares[1].astype(jnp.bfloat16), "seq").astype(jnp.float32),
        lax.psum(shares[2].astype(jnp.bfloat16), "seq").astype(jnp.float32),
        lax.psum(shares[3].astype(jnp.bfloat16), "seq").astype(jnp.float32),
        lax.psum(shares[4].astype(jnp.bfloat16), "seq").astype(jnp.float32),
        lax.psum(shares[5].astype(jnp.bfloat16), "seq").astype(jnp.float32),
        lax.psum(shares[6].astype(jnp.bfloat16), "seq").astype(jnp.float32),
        lax.psum(shares[7].astype(jnp.bfloat16), "seq").astype(jnp.float32),
        lax.psum(shares[8].astype(jnp.bfloat16), "seq").astype(jnp.float32),
        lax.psum(shares[9].astype(jnp.bfloat16), "seq").astype(jnp.float32),
        lax.psum(shares[10].astype(jnp.bfloat16), "seq").astype(jnp.float32),
        lax.psum(shares[11].astype(jnp.bfloat16), "seq").astype(jnp.float32),
    )
    return (
        jnp.stack(outputs),
        jnp.stack(input_grads),
        shares[0],
        shares[1],
        shares[2],
        shares[3],
        shares[4],
        shares[5],
        shares[6],
        shares[7],
        shares[8],
        shares[9],
        shares[10],
        shares[11],
    )


def solution(mesh):
    placed = (
        P(None, "dp", "seq", None),
        P(None, "dp"),
        P("dp"),
        P("dp", None),
        P("dp"),
        P("dp", None),
        P("dp"),
        P("dp", None),
        P("dp"),
        P("dp", None),
        P("dp"),
        P("dp", None),
        P("dp", None),
        P("dp", None),
        P(None, "dp", "seq", None),
    )
    return jax.shard_map(
        per_device,
        mesh=mesh,
        in_specs=placed,
        out_specs=(
            P(None, "dp", "seq", None),
            P(None, "dp", "seq", None),
            P("dp"),
            P("dp", None),
            P("dp"),
            P("dp", None),
            P("dp"),
            P("dp", None),
            P("dp"),
            P("dp", None),
            P("dp"),
            P("dp", None),
            P("dp", None),
            P("dp", None),
        ),
        check_vma=False,
    )
```

profile of v0, /device:TPU:0, one launch (start us, length us, event | category | flops | bytes accessed | tf_op | source)
XLA Modules:
  0.0 1245.0 jit_solution(1288814986106040895)
XLA Ops:
  20.1 42.5 %all-reduce.18 = (bf16[128]{0:T(256)(128)(2,1)S(1)}, bf16[896]{0:T(1024)(128)(2,1)S(1)}, bf16[128]{0:T(256)(128)(2,1)S(1)}, bf16[896]{0:T(1024)(128)(2,1)S(1)}, bf16[896]{0:T(1024)(128)(2,1)S(1)}) all-reduce(bf16[128]{0:T(256)(128)(2,1)S(1)} %dynamic-update-slice.1, ...), channel_id=1, replica_groups=mesh['dp'=16,'seq'=8] {'dp'}, use_global_device_ids=true, to_apply=%add.1 | all-reduce | flops 2944 | bytes 11776
  62.6 21.6 %all_gather.33 = bf16[896,128]{1,0:T(8,128)(2,1)S(1)} all-gather(bf16[56,128]{1,0:T(8,128)(2,1)} %param.22), channel_id=1, replica_groups=mesh['dp'=16,'seq'=8] {'dp'}, dimensions={0}, use_global_device_ids=true | all-gather | bytes 243712 | tf_op jit(solution)/shard_map/all_gather | solution.py:159
  84.7 13.2 %all-gather = bf16[1024,128]{1,0:T(8,128)(2,1)S(1)} all-gather(bf16[128,128]{1,0:T(8,128)(2,1)S(1)} %fusion.60), channel_id=2, replica_groups=mesh['dp'=16,'seq'=8] {'seq'}, dimensions={0}, use_global_device_ids=true | all-gather | bytes 294912 | tf_op jit(solution)/shard_map/all_gather | solution.py:191
  99.0 12.8 %all-gather.2 = bf16[1024,128]{1,0:T(8,128)(2,1)S(1)} all-gather(bf16[128,128]{1,0:T(8,128)(2,1)S(1)} %fusion.61), channel_id=4, replica_groups=mesh['dp'=16,'seq'=8] {'seq'}, dimensions={0}, use_global_device_ids=true | all-gather | bytes 294912 | tf_op jit(solution)/shard_map/all_gather | solution.py:191
  115.0 23.1 %all_gather.36 = bf16[896,128]{1,0:T(8,128)(2,1)S(1)} all-gather(bf16[56,128]{1,0:T(8,128)(2,1)S(1)} %copy-done.68), channel_id=1, replica_groups=mesh['dp'=16,'seq'=8] {'dp'}, dimensions={0}, use_global_device_ids=true | all-gather | bytes 243712 | tf_op jit(solution)/shard_map/all_gather | solution.py:157
  141.4 11.5 all-gather.1
  152.9 13.2 %all-gather.3 = bf16[1024,128]{0,1:T(8,128)(2,1)} all-gather(bf16[128,128]{0,1:T(8,128)(2,1)S(1)} %get-tuple-element.209), channel_id=5, replica_groups=mesh['dp'=16,'seq'=8] {'seq'}, dimensions={0}, use_global_device_ids=true | all-gather | bytes 294912 | tf_op jit(solution)/shard_map/all_gather | solution.py:188
  184.8 2.7 multiply_reduce_fusion.4
  194.2 7.4 convolution_convert_fusion
  201.6 2.5 convolution_convert_fusion.1
  204.1 46.5 %all-gather.16.cloned.1.call-done = bf16[896,4864]{1,0:T(8,128)(2,1)} async-done(((bf16[56,4864]{1,0:T(8,128)(2,1)}), bf16[896,4864]{1,0:T(8,128)(2,1)}) %all-gather.16.cloned.1.call-update) | async-done | bytes 8716304 | tf_op jit(solution)/shard_map/all_gather | solution.py:166
  250.6 4.9 convolution_convert_fusion.4
  255.5 69.0 %all-gather.14.cloned.1.call-done = bf16[896,4864]{1,0:T(8,128)(2,1)} async-done(((bf16[56,4864]{1,0:T(8,128)(2,1)}), bf16[896,4864]{1,0:T(8,128)(2,1)}) %all-gather.14.cloned.1.call-update) | async-done | bytes 8716304 | tf_op jit(solution)/shard_map/all_gather | solution.py:165
  324.6 5.1 convolution_convert_fusion.5
  329.7 7.4 fusion.168
  337.2 4.7 multiply_reduce_fusion.1
  345.2 3.0 fusion.164
  348.2 3.0 multiply_reduce_fusion
  353.7 2.1 convolution_convert_fusion.7
  356.7 7.5 fusion
  364.2 4.6 fusion.2
  370.6 2.9 fusion.53
  376.0 7.7 fusion.3
  383.7 4.6 fusion.5
  390.2 2.9 fusion.52
  395.2 4.6 fusion.49
  401.0 4.4 fusion.46
  408.2 3.2 convolution_add_fusion.3
  412.4 2.9 broadcast_multiply_fusion.2
  418.9 2.4 convolution_add_fusion.4
  422.6 10.4 fusion.166
  433.0 14.6 %convolution_add_fusion.2 = f32[896,4864]{1,0:T(8,128)} fusion(f32[896,4864]{1,0:T(8,128)} %fusion.166, bf16[128,896]{1,0:T(8,128)(2,1)S(1)} %copy-done.26, bf16[128,4864]{1,0:T(8,128)(2,1)S(1)} %copy-done.18, bf16[128,4864]{1,0:T(8,128)(2,1)S(1)} %copy-done.24, bf16[128,4864]{1,0:T(8,128)(2,1)S(1)} %convolution_convert_fusion.3), kind=kOutput, calls=%fused_computation.2 | convolution fusion | flops 1128136704 | bytes 38830080 | tf_op jit(solution)/shard_map/ta,tb->ab/dot_general | solution.py:59
  447.6 4.1 fusion.156
  451.8 10.3 convolution_add_fusion.1
  462.4 4.3 fusion.104
  466.6 10.4 convolution_add_fusion
  480.5 5.3 fusion.59
  493.0 8.2 reduce-scatter.40.cloned.1.call-done
  507.0 74.5 %reduce-scatter.48.cloned.1.call-done = f32[56,896]{1,0:T(8,128)} async-done(((f32[896,896]{1,0:T(8,128)}), f32[56,896]{1,0:T(8,128)}) %reduce-scatter.48.cloned.1.call-update) | async-done | bytes 200720
  583.1 79.3 %reduce-scatter.42.cloned.1.call-done = f32[56,896]{1,0:T(8,128)} async-done(((f32[896,896]{1,0:T(8,128)}), f32[56,896]{1,0:T(8,128)}) %reduce-scatter.42.cloned.1.call-update) | async-done | bytes 200720
  663.9 115.4 %reduce-scatter.50.cloned.1.call-done = f32[56,4864]{1,0:T(8,128)} async-done(((f32[896,4864]{1,0:T(8,128)}), f32[56,4864]{1,0:T(8,128)}) %reduce-scatter.50.cloned.1.call-update) | async-done | bytes 1089552
  781.4 115.7 %reduce-scatter.52.cloned.1.call-done = f32[56,4864]{1,0:T(8,128)} async-done(((f32[896,4864]{1,0:T(8,128)}), f32[56,4864]{1,0:T(8,128)}) %reduce-scatter.52.cloned.1.call-update) | async-done | bytes 1089552
  899.2 115.2 %reduce-scatter.54.cloned.1.call-done = f32[304,896]{1,0:T(8,128)} async-done(((f32[4864,896]{1,0:T(8,128)}), f32[304,896]{1,0:T(8,128)}) %reduce-scatter.54.cloned.1.call-update) | async-done | bytes 1089552
  1016.6 72.3 %all-reduce.17 = (bf16[896]{0:T(1024)(128)(2,1)S(1)}, bf16[896]{0:T(1024)(128)(2,1)S(1)}, bf16[128]{0:T(256)(128)(2,1)S(1)}, bf16[128]{0:T(256)(128)(2,1)S(1)}, bf16[896]{0:T(1024)(128)(2,1)S(1)}) all-reduce(f32[896]{0:T(1024)S(1)} %add.367, f32[896]{0:T(1024)S(1)} %add.372, ...), channel_id=10, replica_groups=mesh['dp'=16,'seq'=8] {'dp'}, use_global_device_ids=true, to_apply=%region_20.21.clone | all-reduce | flops 2944 | bytes 17664
  1091.3 71.1 %reduce-scatter.44.cloned.1.call-done = f32[56,128]{1,0:T(8,128)} async-done(((f32[896,128]{1,0:T(8,128)}), f32[56,128]{1,0:T(8,128)}) %reduce-scatter.44.cloned.1.call-update) | async-done | bytes 28688
  1163.1 23.7 %all-reduce.19 = (bf16[56]{0:T(256)(128)(2,1)S(1)}, bf16[56]{0:T(256)(128)(2,1)S(1)}, bf16[56,128]{1,0:T(8,128)(2,1)S(1)}, bf16[8]{0:T(256)(128)(2,1)S(1)}, bf16...) all-reduce(bf16[56]{0:T(256)(128)(2,1)S(1)} %dynamic-slice.44, ...), channel_id=1, replica_groups=mesh['dp'=16,'seq'=8] {'seq'}, use_global_device_ids=true, to_apply=%region_21.22 | all-reduce | flops 14520 | bytes 58080 | tf_op jit(solution)/shard_map/psum | solution.py:324
  1190.6 40.1 %all-reduce.23.cloned.1.call-done = (bf16[56,896]{1,0:T(8,128)(2,1)}, bf16[56,896]{1,0:T(8,128)(2,1)}, bf16[56,4864]{1,0:T(8,128)(2,1)}, bf16[56,4864]{1,0:T(8,128)(2,1)}, bf16[304,896]{1,0:T(8,128)(2,1)}) async-done(((bf16[56,896]{1,0:T(8,128)(2,1)}, bf16[56,896]{1,0:T(8,128)(2,1)}, bf16[56,4864]{1,0:T(8,128)(2,1)}, bf16[56,4864]{1,0:T(8,128)(2,1)}, bf16[304,896]{1,0:T(8,128)(2,1)}), ...) | async-done | bytes 1835024 | tf_op jit(solution)/shard_map/psum | solution.py:325
  1234.0 2.1 convert_element_type.548
  (368 shorter events, 104.3 us)
Async XLA Ops:
  7.2 77.0 %copy-start.12 = (bf16[2,1,128,896]{3,2,1,0:T(8,128)(2,1)S(1)}, bf16[2,1,128,896]{3,2,1,0:T(8,128)(2,1)}, u32[]{:S(2)}) copy-start(bf16[2,1,128,896]{3,2,1,0:T(8,128)(2,1)} %param.15) | copy-start | bytes 1376260
  7.2 160.0 %all-gather.10.cloned.1.call-start = ((), (), s32[]{:S(2)}) async-start(), calls=%async_computation.11 | async-start | bytes 1705984 | tf_op jit(solution)/shard_map/all_gather | solution.py:155
  7.9 176.9 %all-gather.12.cloned.1.call-start = ((), (), s32[]{:S(2)}) async-start(), calls=%async_computation.12 | async-start | bytes 1705984 | tf_op jit(solution)/shard_map/all_gather | solution.py:161
  8.7 185.2 %all-gather.18.cloned.1.call-start = ((), (), s32[]{:S(2)}) async-start(), calls=%async_computation.15 | async-start | bytes 9261056 | tf_op jit(solution)/shard_map/all_gather | solution.py:167
  9.4 241.2 %all-gather.16.cloned.1.call-start = ((), (), s32[]{:S(2)}) async-start(), calls=%async_computation.14 | async-start | bytes 9261056 | tf_op jit(solution)/shard_map/all_gather | solution.py:166
  10.0 314.6 %all-gather.14.cloned.1.call-start = ((), (), s32[]{:S(2)}) async-start(), calls=%async_computation.13 | async-start | bytes 9261056 | tf_op jit(solution)/shard_map/all_gather | solution.py:165
  10.6 479.5 %reduce-scatter.38.cloned.1.call-start = ((), (), s32[]{:S(2)}) async-start(), calls=%async_computation.18 | async-start | bytes 294912
  84.2 28.5 %copy-start.63 = (bf16[896,128]{1,0:T(8,128)(2,1)}, bf16[896,128]{1,0:T(8,128)(2,1)S(1)}, u32[]{:S(2)}) copy-start(bf16[896,128]{1,0:T(8,128)(2,1)S(1)} %all_gather.33) | copy-start | bytes 688132
  97.9 17.1 %copy-start.68 = (bf16[56,128]{1,0:T(8,128)(2,1)S(1)}, bf16[56,128]{1,0:T(8,128)(2,1)}, u32[]{:S(2)}) copy-start(bf16[56,128]{1,0:T(8,128)(2,1)} %param.20) | copy-start | bytes 43012
  112.9 25.9 %copy-start.54 = (f32[128,64]{0,1:T(8,128)}, f32[128,64]{0,1:T(8,128)S(1)}, u32[]{:S(2)}) copy-start(f32[128,64]{0,1:T(8,128)S(1)} %get-tuple-element.216) | copy-start | bytes 98308
  112.9 25.9 %copy-start.56 = (f32[128,64]{0,1:T(8,128)}, f32[128,64]{0,1:T(8,128)S(1)}, u32[]{:S(2)}) copy-start(f32[128,64]{0,1:T(8,128)S(1)} %get-tuple-element.217) | copy-start | bytes 98308
  152.9 34.6 %copy-start.40 = (bf16[1024,128]{0,1:T(8,128)(2,1)}, bf16[1024,128]{0,1:T(8,128)(2,1)S(1)}, u32[]{:S(2)}) copy-start(bf16[1024,128]{0,1:T(8,128)(2,1)S(1)} %all-gather.1) | copy-start | bytes 786436
  179.0 8.6 copy-start.48
  193.1 8.6 copy-start.65
  193.7 8.0 copy-start.38
  194.2 7.4 copy-start.2
  204.1 133.1 %copy-start.22 = (bf16[128,4864]{1,0:T(8,128)(2,1)}, bf16[128,4864]{1,0:T(8,128)(2,1)S(1)}, u32[]{:S(2)}) copy-start(bf16[128,4864]{1,0:T(8,128)(2,1)S(1)} %convolution_convert_fusion.1) | copy-start | bytes 3735556
  255.5 74.1 %copy-start.20 = (bf16[128,4864]{1,0:T(8,128)(2,1)}, bf16[128,4864]{1,0:T(8,128)(2,1)S(1)}, u32[]{:S(2)}) copy-start(bf16[128,4864]{1,0:T(8,128)(2,1)S(1)} %convolution_convert_fusion.4) | copy-start | bytes 3735556
  324.5 12.6 %slice-start.4 = ((s8[8716288]{0:T(1024)(128)(4,1)}), s8[4194304]{0:T(1024)(128)(4,1)S(1)}, s32[]{:S(2)}) async-start(s8[8716288]{0:T(1024)(128)(4,1)} %bitcast.431), calls=%async_computation.32 | async-start | bytes 8388608
  324.5 12.6 %slice-start.5 = ((s8[8716288]{0:T(1024)(128)(4,1)}), s8[4194304]{0:T(1024)(128)(4,1)S(1)}, s32[]{:S(2)}) async-start(s8[8716288]{0:T(1024)(128)(4,1)} %bitcast.431), calls=%async_computation.33 | async-start | bytes 8388608
  329.7 7.5 copy-start.14
  329.7 7.5 slice-start.6
  329.7 7.5 copy-start.39
  329.7 7.5 copy-start.52
  345.2 87.7 %copy-start.6 = (bf16[128,4864]{1,0:T(8,128)(2,1)}, bf16[128,4864]{1,0:T(8,128)(2,1)S(1)}, u32[]{:S(2)}) copy-start(bf16[128,4864]{1,0:T(8,128)(2,1)S(1)} %convolution_convert_fusion.3) | copy-start | bytes 3735556
  353.7 10.4 copy-start.44
  356.7 7.5 slice-start
  356.7 7.5 slice-start.1
  375.5 115.5 %reduce-scatter.34.cloned.1.call-start = ((), (), s32[]{:S(2)}) async-start(), calls=%async_computation.16 | async-start | bytes 294912
  376.0 7.7 slice-start.2
  376.0 7.7 slice-start.3
  395.1 96.9 %reduce-scatter.36.cloned.1.call-start = ((), (), s32[]{:S(2)}) async-start(), calls=%async_computation.17 | async-start | bytes 294912
  400.9 100.2 %reduce-scatter.40.cloned.1.call-start = ((), (), s32[]{:S(2)}) async-start(), calls=%async_computation.19 | async-start | bytes 294912
  406.6 174.9 %reduce-scatter.48.cloned.1.call-start = ((), (), s32[]{:S(2)}) async-start(), calls=%async_computation.23 | async-start | bytes 3411968
  411.4 250.9 %reduce-scatter.42.cloned.1.call-start = ((), (), s32[]{:S(2)}) async-start(), calls=%async_computation.20 | async-start | bytes 3411968
  421.3 11.7 copy-start.26
  421.3 358.0 %reduce-scatter.50.cloned.1.call-start = ((), (), s32[]{:S(2)}) async-start(), calls=%async_computation.24 | async-start | bytes 18522112
  422.6 10.4 copy-start.18
  422.6 10.4 copy-start.24
  447.6 449.5 %reduce-scatter.52.cloned.1.call-start = ((), (), s32[]{:S(2)}) async-start(), calls=%async_computation.25 | async-start | bytes 18522112
  462.1 552.2 %reduce-scatter.54.cloned.1.call-start = ((), (), s32[]{:S(2)}) async-start(), calls=%async_computation.26 | async-start | bytes 18522112
  477.1 8.8 slice-start.10
  477.1 613.5 %reduce-scatter.46.cloned.1.call-start = ((), (), s32[]{:S(2)}) async-start(), calls=%async_computation.22 | async-start | bytes 487424
  488.9 13.3 %copy-start.13 = (bf16[2,1,128,896]{3,2,1,0:T(8,128)(2,1)S(1)}, bf16[2,1,128,896]{3,2,1,0:T(8,128)(2,1)}, u32[]{:S(2)}) copy-start(bf16[2,1,128,896]{3,2,1,0:T(8,128)(2,1)} %param.15) | copy-start | bytes 1376260
  503.6 658.8 %reduce-scatter.44.cloned.1.call-start = ((), (), s32[]{:S(2)}) async-start(), calls=%async_computation.21 | async-start | bytes 487424
  505.3 725.4 %all-reduce.23.cloned.1.call-start = ((), (), s32[]{:S(2)}) async-start(), calls=%async_computation.27 | async-start | bytes 3670016 | tf_op jit(solution)/shard_map/psum | solution.py:325
  781.4 307.9 %copy-start.29 = (f32[128,896]{1,0:T(8,128)S(1)}, f32[128,896]{1,0:T(8,128)}, u32[]{:S(2)}) copy-start(f32[128,896]{1,0:T(8,128)} %copy-done.27) | copy-start | bytes 1376260
  781.4 307.9 %copy-start.32 = (f32[128,896]{1,0:T(8,128)S(1)}, f32[128,896]{1,0:T(8,128)}, u32[]{:S(2)}) copy-start(f32[128,896]{1,0:T(8,128)} %copy-done.30) | copy-start | bytes 1376260
  (52 other events, 173.6 us)
Sparse Core Ops, SparseCore 0:
  10.2 46.6 all-gather.9
  59.0 43.4 all-gather.11
  104.7 71.8 all-gather.17
  178.6 71.9 all-gather.15
  252.6 71.9 all-gather.13
  375.7 30.0 reduce-scatter.37
  408.3 29.3 reduce-scatter.33
  440.0 29.3 reduce-scatter.35
  471.8 29.3 reduce-scatter.39
  504.5 76.9 reduce-scatter.47
  585.0 77.3 reduce-scatter.41
  665.7 113.5 reduce-scatter.49
  783.1 113.8 reduce-scatter.51
  900.4 113.9 reduce-scatter.53
  1017.7 70.8 reduce-scatter.45
  1091.7 70.6 reduce-scatter.43
  1166.3 64.3 all-reduce.22
where the time goes:
time: 1250 us; the launch traced here: 1240 us
  waiting for transfers between devices  738 us (59%)
  blocking collectives  234 us (19%)
  matrix products  164 us (13%)
  other arithmetic  48 us (4%)
  local copies, waits for them, and re-layouts  39.6 us (3%)
  between operations  19.9 us (2%)
    unnamed x28, waiting for transfers between devices  583 us
    unnamed x2, blocking collectives  115 us
    all_gather x1, waiting for transfers between devices, per_device(): lax.all_gather(w_gate, 'dp', axis=0, tiled=True)  69 us
    dot_general x14, matrix products, outer_sum(): jnp.einsum('ta,tb->ab', left, right, preferred_element_type=jnp.float32)  64.8 us
    all_gather x1, waiting for transfers between devices, per_device(): lax.all_gather(w_up, 'dp', axis=0, tiled=True)  46.5 us
    psum x1, waiting for transfers between devices, per_device(): lax.psum(shares[1].astype(jnp.bfloat16), 'seq').astype(jnp.float32)  40.1 us
    dot_general x14, matrix products, back_dot(): jnp.einsum('tb,ab->ta', grad_rows, weight, preferred_element_type=jnp.flo...  33.1 us
    unnamed x198, local copies, waits for them, and re-layouts  28 us
  transfers between devices with their start and end apart: 17, of which 10 were waited for; matrix products, arithmetic and copies ran while one was open for 15% of the time, Pallas kernels for 0%

commit v1 on v0

--- a/solution.py
+++ b/solution.py
@@ -10,6 +10,27 @@
 EPSILON = 1e-06
 ROPE_BASE = 1000000.0
 NEGATIVE = -1e30
+
+
+def ring_gather(shard, axis, dim):
+    count, here, rows = (lax.axis_size(axis), lax.axis_index(axis), shard.shape[dim])
+    upward = [(i, (i + 1) % count) for i in range(count)]
+    behind = [(i, (i - 1) % count) for i in range(count)]
+    out = jnp.zeros((*shard.shape[:dim], count * rows, *shard.shape[dim + 1 :]), shard.dtype)
+    out = lax.dynamic_update_slice_in_dim(out, shard, here * rows, axis=dim)
+    from_left = from_right = shard
+    half = count // 2
+    for step in range(1, half + 1):
+        from_left = lax.ppermute(from_left, axis, upward)
+        out = lax.dynamic_update_slice_in_dim(
+            out, from_left, (here - step) % count * rows, axis=dim
+        )
+        if step < count - half:
+            from_right = lax.ppermute(from_right, axis, behind)
+            out = lax.dynamic_update_slice_in_dim(
+                out, from_right, (here + step) % count * rows, axis=dim
+            )
+    return out
 
 
 def rope_tables(positions, head_dim):
@@ -188,9 +209,7 @@
             lax.all_gather(
                 keys.reshape(seq_count, row_count, KV_HEADS * HD), "seq", axis=1, tiled=True
             ),
-            lax.all_gather(
-                values.reshape(seq_count, row_count, KV_HEADS * HD), "seq", axis=1, tiled=True
-            ),
+            ring_gather(values.reshape(seq_count, row_count, KV_HEADS * HD), "seq", 1),
         )
         query_seqs = queries.reshape(seq_count, row_count, HEADS * HD)
         starts = pic_start[micro_index]

time: 1250 us -> 1250 us (level)
  blocking collectives: 234 us -> 208 us
  starting transfers between devices: 1.73 us -> 14.8 us
  waiting for transfers between devices: 738 us -> 751 us
    all_gather x2 -> x0, blocking collectives: 26 us -> none  [per_device(): lax.all_gather(values.reshape(seq_count, row_count, KV_HEADS * HD), 'seq'...]
    ppermute x0 -> x14, starting transfers between devices: none -> 13.1 us  [the longest x6 12.6 us: ring_gather(): from_right = lax.ppermute(from_right, axis, behind)]
    unnamed x198 -> x204, local copies, waits for them, and re-layouts: 28 us -> 28.5 us
  transfers between devices with their start and end apart: 17 -> 31, of which waited for: 10 -> 14; matrix products, arithmetic and copies ran while one was open for 15% -> 15% of each run, Pallas kernels for 0% -> 0%
where the time goes in v1:
time: 1250 us; the launch traced here: 1240 us
  waiting for transfers between devices  751 us (60%)
  blocking collectives  208 us (17%)
  matrix products  164 us (13%)
  other arithmetic  49.2 us (4%)
  local copies, waits for them, and re-layouts  37.9 us (3%)
  between operations  20.1 us (2%)
  starting transfers between devices  14.8 us (1%)
    unnamed x28, waiting for transfers between devices  583 us
    unnamed x2, blocking collectives  115 us
    all_gather x1, waiting for transfers between devices, per_device(): lax.all_gather(w_gate, 'dp', axis=0, tiled=True)  69 us
    dot_general x14, matrix products, outer_sum(): jnp.einsum('ta,tb->ab', left, right, preferred_element_type=jnp.float32)  64.8 us
    all_gather x1, waiting for transfers between devices, per_device(): lax.all_gather(w_up, 'dp', axis=0, tiled=True)  50.5 us
    psum x1, waiting for transfers between devices, per_device(): lax.psum(shares[1].astype(jnp.bfloat16), 'seq').astype(jnp.float32)  40 us
    dot_general x14, matrix products, back_dot(): jnp.einsum('tb,ab->ta', grad_rows, weight, preferred_element_type=jnp.flo...  32.7 us
    unnamed x204, local copies, waits for them, and re-layouts  28.5 us
  transfers between devices with their start and end apart: 31, of which 14 were waited for; matrix products, arithmetic and copies ran while one was open for 15% of the time, Pallas kernels for 0%

profile of v1, /device:TPU:0, one launch (start us, length us, event | category | flops | bytes accessed | tf_op | source)
XLA Modules:
  0.0 1244.7 jit_solution(11971223825559390602)
XLA Ops:
  17.5 42.5 %all-reduce.18 = (bf16[128]{0:T(256)(128)(2,1)S(1)}, bf16[896]{0:T(1024)(128)(2,1)S(1)}, bf16[128]{0:T(256)(128)(2,1)S(1)}, bf16[896]{0:T(1024)(128)(2,1)S(1)}, bf16[896]{0:T(1024)(128)(2,1)S(1)}) all-reduce(bf16[128]{0:T(256)(128)(2,1)S(1)} %dynamic-update-slice.1, ...), channel_id=1, replica_groups=mesh['dp'=16,'seq'=8] {'dp'}, use_global_device_ids=true, to_apply=%add.1 | all-reduce | flops 2944 | bytes 11776
  60.0 21.4 %all_gather.29 = bf16[896,128]{1,0:T(8,128)(2,1)S(1)} all-gather(bf16[56,128]{1,0:T(8,128)(2,1)} %param.22), channel_id=1, replica_groups=mesh['dp'=16,'seq'=8] {'dp'}, dimensions={0}, use_global_device_ids=true | all-gather | bytes 243712 | tf_op jit(solution)/shard_map/all_gather | solution.py:180
  84.0 2.7 collective-permute-start.1
  88.7 23.3 %all_gather.31 = bf16[896,128]{1,0:T(8,128)(2,1)S(1)} all-gather(bf16[56,128]{1,0:T(8,128)(2,1)S(1)} %copy-done.70), channel_id=1, replica_groups=mesh['dp'=16,'seq'=8] {'dp'}, dimensions={0}, use_global_device_ids=true | all-gather | bytes 243712 | tf_op jit(solution)/shard_map/all_gather | solution.py:178
  115.6 11.5 all-gather
  128.1 13.2 %all-gather.1 = bf16[1024,128]{0,1:T(8,128)(2,1)} all-gather(bf16[128,128]{0,1:T(8,128)(2,1)S(1)} %get-tuple-element.209), channel_id=3, replica_groups=mesh['dp'=16,'seq'=8] {'seq'}, dimensions={0}, use_global_device_ids=true | all-gather | bytes 294912 | tf_op jit(solution)/shard_map/all_gather | solution.py:209
  144.3 3.0 collective-permute-start.3
  147.4 3.0 collective-permute-start.12
  150.4 3.0 collective-permute-start.5
  154.9 3.0 collective-permute-done.4
  159.5 2.9 collective-permute-done.6
  180.9 2.7 multiply_reduce_fusion.4
  190.3 7.3 convolution_convert_fusion
  200.1 50.5 %all-gather.14.cloned.1.call-done = bf16[896,4864]{1,0:T(8,128)(2,1)} async-done(((bf16[56,4864]{1,0:T(8,128)(2,1)}), bf16[896,4864]{1,0:T(8,128)(2,1)}) %all-gather.14.cloned.1.call-update) | async-done | bytes 8716304 | tf_op jit(solution)/shard_map/all_gather | solution.py:187
  250.5 4.9 convolution_convert_fusion.4
  255.5 69.0 %all-gather.12.cloned.1.call-done = bf16[896,4864]{1,0:T(8,128)(2,1)} async-done(((bf16[56,4864]{1,0:T(8,128)(2,1)}), bf16[896,4864]{1,0:T(8,128)(2,1)}) %all-gather.12.cloned.1.call-update) | async-done | bytes 8716304 | tf_op jit(solution)/shard_map/all_gather | solution.py:186
  324.5 5.1 convolution_convert_fusion.5
  329.7 7.4 fusion.168
  337.2 4.7 multiply_reduce_fusion.1
  345.2 2.7 fusion.164
  348.0 3.0 multiply_reduce_fusion
  356.4 7.5 fusion
  363.9 4.6 fusion.2
  370.3 2.9 fusion.53
  375.7 7.7 fusion.3
  383.5 4.6 fusion.5
  389.9 2.9 fusion.52
  394.9 4.6 fusion.49
  400.8 4.4 fusion.46
  407.9 3.2 convolution_add_fusion.3
  412.1 2.9 broadcast_multiply_fusion.2
  422.3 10.3 fusion.166
  432.7 14.6 %convolution_add_fusion.2 = f32[896,4864]{1,0:T(8,128)} fusion(f32[896,4864]{1,0:T(8,128)} %fusion.166, bf16[128,896]{1,0:T(8,128)(2,1)S(1)} %copy-done.26, bf16[128,4864]{1,0:T(8,128)(2,1)S(1)} %copy-done.18, bf16[128,4864]{1,0:T(8,128)(2,1)S(1)} %copy-done.24, bf16[128,4864]{1,0:T(8,128)(2,1)S(1)} %convolution_convert_fusion.3), kind=kOutput, calls=%fused_computation.2 | convolution fusion | flops 1128136704 | bytes 38830080 | tf_op jit(solution)/shard_map/ta,tb->ab/dot_general | solution.py:80
  447.3 4.1 fusion.156
  451.5 10.3 convolution_add_fusion.1
  462.1 4.3 fusion.104
  466.4 10.4 convolution_add_fusion
  480.2 5.3 fusion.59
  492.7 8.2 reduce-scatter.40.cloned.1.call-done
  506.7 74.4 %reduce-scatter.48.cloned.1.call-done = f32[56,896]{1,0:T(8,128)} async-done(((f32[896,896]{1,0:T(8,128)}), f32[56,896]{1,0:T(8,128)}) %reduce-scatter.48.cloned.1.call-update) | async-done | bytes 200720
  582.8 79.3 %reduce-scatter.42.cloned.1.call-done = f32[56,896]{1,0:T(8,128)} async-done(((f32[896,896]{1,0:T(8,128)}), f32[56,896]{1,0:T(8,128)}) %reduce-scatter.42.cloned.1.call-update) | async-done | bytes 200720
  663.7 115.4 %reduce-scatter.50.cloned.1.call-done = f32[56,4864]{1,0:T(8,128)} async-done(((f32[896,4864]{1,0:T(8,128)}), f32[56,4864]{1,0:T(8,128)}) %reduce-scatter.50.cloned.1.call-update) | async-done | bytes 1089552
  781.2 115.7 %reduce-scatter.52.cloned.1.call-done = f32[56,4864]{1,0:T(8,128)} async-done(((f32[896,4864]{1,0:T(8,128)}), f32[56,4864]{1,0:T(8,128)}) %reduce-scatter.52.cloned.1.call-update) | async-done | bytes 1089552
  898.9 115.2 %reduce-scatter.54.cloned.1.call-done = f32[304,896]{1,0:T(8,128)} async-done(((f32[4864,896]{1,0:T(8,128)}), f32[304,896]{1,0:T(8,128)}) %reduce-scatter.54.cloned.1.call-update) | async-done | bytes 1089552
  1016.4 72.3 %all-reduce.17 = (bf16[896]{0:T(1024)(128)(2,1)S(1)}, bf16[896]{0:T(1024)(128)(2,1)S(1)}, bf16[128]{0:T(256)(128)(2,1)S(1)}, bf16[128]{0:T(256)(128)(2,1)S(1)}, bf16[896]{0:T(1024)(128)(2,1)S(1)}) all-reduce(f32[896]{0:T(1024)S(1)} %add.462, f32[896]{0:T(1024)S(1)} %add.467, ...), channel_id=8, replica_groups=mesh['dp'=16,'seq'=8] {'dp'}, use_global_device_ids=true, to_apply=%region_20.21.clone | all-reduce | flops 2944 | bytes 17664
  1091.1 71.1 %reduce-scatter.44.cloned.1.call-done = f32[56,128]{1,0:T(8,128)} async-done(((f32[896,128]{1,0:T(8,128)}), f32[56,128]{1,0:T(8,128)}) %reduce-scatter.44.cloned.1.call-update) | async-done | bytes 28688
  1162.9 23.7 %all-reduce.19 = (bf16[56]{0:T(256)(128)(2,1)S(1)}, bf16[56]{0:T(256)(128)(2,1)S(1)}, bf16[56,128]{1,0:T(8,128)(2,1)S(1)}, bf16[8]{0:T(256)(128)(2,1)S(1)}, bf16...) all-reduce(bf16[56]{0:T(256)(128)(2,1)S(1)} %dynamic-slice.44, ...), channel_id=1, replica_groups=mesh['dp'=16,'seq'=8] {'seq'}, use_global_device_ids=true, to_apply=%region_21.22 | all-reduce | flops 14520 | bytes 58080 | tf_op jit(solution)/shard_map/psum | solution.py:343
  1190.4 40.0 %all-reduce.23.cloned.1.call-done = (bf16[56,896]{1,0:T(8,128)(2,1)}, bf16[56,896]{1,0:T(8,128)(2,1)}, bf16[56,4864]{1,0:T(8,128)(2,1)}, bf16[56,4864]{1,0:T(8,128)(2,1)}, bf16[304,896]{1,0:T(8,128)(2,1)}) async-done(((bf16[56,896]{1,0:T(8,128)(2,1)}, bf16[56,896]{1,0:T(8,128)(2,1)}, bf16[56,4864]{1,0:T(8,128)(2,1)}, bf16[56,4864]{1,0:T(8,128)(2,1)}, bf16[304,896]{1,0:T(8,128)(2,1)}), ...) | async-done | bytes 1835024 | tf_op jit(solution)/shard_map/psum | solution.py:344
  (414 shorter events, 117.7 us)
Async XLA Ops:
  7.2 75.6 %copy-start.12 = (bf16[2,1,128,896]{3,2,1,0:T(8,128)(2,1)S(1)}, bf16[2,1,128,896]{3,2,1,0:T(8,128)(2,1)}, u32[]{:S(2)}) copy-start(bf16[2,1,128,896]{3,2,1,0:T(8,128)(2,1)} %param.15) | copy-start | bytes 1376260
  7.2 79.6 %copy-start.72 = (s32[2,1]{0,1:T(1,128)S(1)}, s32[2,1]{0,1:T(1,128)}, u32[]{:S(2)}) copy-start(s32[2,1]{0,1:T(1,128)} %param.16) | copy-start | bytes 28
  7.2 81.4 %copy-start.70 = (bf16[56,128]{1,0:T(8,128)(2,1)S(1)}, bf16[56,128]{1,0:T(8,128)(2,1)}, u32[]{:S(2)}) copy-start(bf16[56,128]{1,0:T(8,128)(2,1)} %param.20) | copy-start | bytes 43012
  7.2 156.0 %all-gather.8.cloned.1.call-start = ((), (), s32[]{:S(2)}) async-start(), calls=%async_computation.11 | async-start | bytes 1705984 | tf_op jit(solution)/shard_map/all_gather | solution.py:176
  7.9 172.9 %all-gather.10.cloned.1.call-start = ((), (), s32[]{:S(2)}) async-start(), calls=%async_computation.12 | async-start | bytes 1705984 | tf_op jit(solution)/shard_map/all_gather | solution.py:182
  8.7 181.3 %all-gather.16.cloned.1.call-start = ((), (), s32[]{:S(2)}) async-start(), calls=%async_computation.15 | async-start | bytes 9261056 | tf_op jit(solution)/shard_map/all_gather | solution.py:188
  9.4 241.1 %all-gather.14.cloned.1.call-start = ((), (), s32[]{:S(2)}) async-start(), calls=%async_computation.14 | async-start | bytes 9261056 | tf_op jit(solution)/shard_map/all_gather | solution.py:187
  10.0 314.5 %all-gather.12.cloned.1.call-start = ((), (), s32[]{:S(2)}) async-start(), calls=%async_computation.13 | async-start | bytes 9261056 | tf_op jit(solution)/shard_map/all_gather | solution.py:186
  10.6 479.2 %reduce-scatter.38.cloned.1.call-start = ((), (), s32[]{:S(2)}) async-start(), calls=%async_computation.18 | async-start | bytes 294912
  81.4 31.5 %copy-start.65 = (bf16[896,128]{1,0:T(8,128)(2,1)}, bf16[896,128]{1,0:T(8,128)(2,1)S(1)}, u32[]{:S(2)}) copy-start(bf16[896,128]{1,0:T(8,128)(2,1)S(1)} %all_gather.29) | copy-start | bytes 688132
  83.1 60.2 %collective-permute-start.8 = (bf16[1,128,128]{1,2,0:T(8,128)(2,1)S(1)}, bf16[1,128,128]{1,2,0:T(8,128)(2,1)S(1)}, u32[]{:S(2)}, u32[]{:S(2)}) collective-permute-start(bf16[1,128,128]{1,2,0:T(8,128)(2,1)S(1)} %bitcast.523), channel_id=1, source_target_pairs={{0,7},{1,0},{2,1},{3,2},{4,3},{5,4},{6,5},{7,6},{8,15},{9,8},{10,9... | collective-permute-start | bytes 98312 | tf_op jit(solution)/shard_map/ppermute | solution.py:29
  83.1 61.2 %collective-permute-start.7 = (bf16[1,128,128]{1,2,0:T(8,128)(2,1)S(1)}, bf16[1,128,128]{1,2,0:T(8,128)(2,1)S(1)}, u32[]{:S(2)}, u32[]{:S(2)}) collective-permute-start(bf16[1,128,128]{1,2,0:T(8,128)(2,1)S(1)} %bitcast.524), channel_id=1, source_target_pairs={{0,1},{1,2},{2,3},{3,4},{4,5},{5,6},{6,7},{7,0},{8,9},{9,10},{10,1... | collective-permute-start | bytes 98312 | tf_op jit(solution)/shard_map/ppermute | solution.py:24
  84.0 60.3 %collective-permute-start.1 = (bf16[1,128,128]{1,2,0:T(8,128)(2,1)S(1)}, bf16[1,128,128]{1,2,0:T(8,128)(2,1)S(1)}, u32[]{:S(2)}, u32[]{:S(2)}) collective-permute-start(bf16[1,128,128]{1,2,0:T(8,128)(2,1)S(1)} %bitcast.525), channel_id=1, source_target_pairs={{0,7},{1,0},{2,1},{3,2},{4,3},{5,4},{6,5},{7,6},{8,15},{9,8},{10,9... | collective-permute-start | bytes 98312 | tf_op jit(solution)/shard_map/ppermute | solution.py:29
  86.7 60.5 %collective-permute-start = (bf16[1,128,128]{1,2,0:T(8,128)(2,1)S(1)}, bf16[1,128,128]{1,2,0:T(8,128)(2,1)S(1)}, u32[]{:S(2)}, u32[]{:S(2)}) collective-permute-start(bf16[1,128,128]{1,2,0:T(8,128)(2,1)S(1)} %bitcast.526), channel_id=1, source_target_pairs={{0,1},{1,2},{2,3},{3,4},{4,5},{5,6},{6,7},{7,0},{8,9},{9,10},{10,1... | collective-permute-start | bytes 98312 | tf_op jit(solution)/shard_map/ppermute | solution.py:24
  112.9 45.1 %copy-start.54 = (f32[128,64]{0,1:T(8,128)}, f32[128,64]{0,1:T(8,128)S(1)}, u32[]{:S(2)}) copy-start(f32[128,64]{0,1:T(8,128)S(1)} %get-tuple-element.216) | copy-start | bytes 98308
  112.9 45.1 %copy-start.56 = (f32[128,64]{0,1:T(8,128)}, f32[128,64]{0,1:T(8,128)S(1)}, u32[]{:S(2)}) copy-start(f32[128,64]{0,1:T(8,128)S(1)} %get-tuple-element.217) | copy-start | bytes 98308
  127.1 56.5 %copy-start.40 = (bf16[1024,128]{0,1:T(8,128)(2,1)}, bf16[1024,128]{0,1:T(8,128)(2,1)S(1)}, u32[]{:S(2)}) copy-start(bf16[1024,128]{0,1:T(8,128)(2,1)S(1)} %all-gather) | copy-start | bytes 786436
  143.3 4.0 collective-permute-start.10
  144.3 6.0 collective-permute-start.9
  144.3 6.0 collective-permute-start.3
  147.3 6.0 collective-permute-start.2
  147.4 10.5 collective-permute-start.12
  150.4 4.6 collective-permute-start.11
  150.4 7.6 collective-permute-start.5
  153.3 4.6 collective-permute-start.4
  154.9 4.6 collective-permute-start.13
  157.9 4.6 collective-permute-start.6
  200.0 137.1 %copy-start.22 = (bf16[128,4864]{1,0:T(8,128)(2,1)}, bf16[128,4864]{1,0:T(8,128)(2,1)S(1)}, u32[]{:S(2)}) copy-start(bf16[128,4864]{1,0:T(8,128)(2,1)S(1)} %convolution_convert_fusion.1) | copy-start | bytes 3735556
  255.5 74.1 %copy-start.20 = (bf16[128,4864]{1,0:T(8,128)(2,1)}, bf16[128,4864]{1,0:T(8,128)(2,1)S(1)}, u32[]{:S(2)}) copy-start(bf16[128,4864]{1,0:T(8,128)(2,1)S(1)} %convolution_convert_fusion.4) | copy-start | bytes 3735556
  324.5 12.6 %slice-start.4 = ((s8[8716288]{0:T(1024)(128)(4,1)}), s8[4194304]{0:T(1024)(128)(4,1)S(1)}, s32[]{:S(2)}) async-start(s8[8716288]{0:T(1024)(128)(4,1)} %bitcast.465), calls=%async_computation.32 | async-start | bytes 8388608
  324.5 12.6 %slice-start.5 = ((s8[8716288]{0:T(1024)(128)(4,1)}), s8[4194304]{0:T(1024)(128)(4,1)S(1)}, s32[]{:S(2)}) async-start(s8[8716288]{0:T(1024)(128)(4,1)} %bitcast.465), calls=%async_computation.33 | async-start | bytes 8388608
  345.2 87.5 %copy-start.6 = (bf16[128,4864]{1,0:T(8,128)(2,1)}, bf16[128,4864]{1,0:T(8,128)(2,1)S(1)}, u32[]{:S(2)}) copy-start(bf16[128,4864]{1,0:T(8,128)(2,1)S(1)} %convolution_convert_fusion.3) | copy-start | bytes 3735556
  353.4 10.5 copy-start.44
  375.3 115.5 %reduce-scatter.34.cloned.1.call-start = ((), (), s32[]{:S(2)}) async-start(), calls=%async_computation.16 | async-start | bytes 294912
  394.9 96.9 %reduce-scatter.36.cloned.1.call-start = ((), (), s32[]{:S(2)}) async-start(), calls=%async_computation.17 | async-start | bytes 294912
  400.7 100.2 %reduce-scatter.40.cloned.1.call-start = ((), (), s32[]{:S(2)}) async-start(), calls=%async_computation.19 | async-start | bytes 294912
  406.3 174.9 %reduce-scatter.48.cloned.1.call-start = ((), (), s32[]{:S(2)}) async-start(), calls=%async_computation.23 | async-start | bytes 3411968
  411.2 250.9 %reduce-scatter.42.cloned.1.call-start = ((), (), s32[]{:S(2)}) async-start(), calls=%async_computation.20 | async-start | bytes 3411968
  421.1 11.6 copy-start.26
  421.1 358.0 %reduce-scatter.50.cloned.1.call-start = ((), (), s32[]{:S(2)}) async-start(), calls=%async_computation.24 | async-start | bytes 18522112
  447.3 449.5 %reduce-scatter.52.cloned.1.call-start = ((), (), s32[]{:S(2)}) async-start(), calls=%async_computation.25 | async-start | bytes 18522112
  461.8 552.3 %reduce-scatter.54.cloned.1.call-start = ((), (), s32[]{:S(2)}) async-start(), calls=%async_computation.26 | async-start | bytes 18522112
  476.8 613.5 %reduce-scatter.46.cloned.1.call-start = ((), (), s32[]{:S(2)}) async-start(), calls=%async_computation.22 | async-start | bytes 487424
  488.6 13.3 %copy-start.13 = (bf16[2,1,128,896]{3,2,1,0:T(8,128)(2,1)S(1)}, bf16[2,1,128,896]{3,2,1,0:T(8,128)(2,1)}, u32[]{:S(2)}) copy-start(bf16[2,1,128,896]{3,2,1,0:T(8,128)(2,1)} %param.15) | copy-start | bytes 1376260
  503.4 658.8 %reduce-scatter.44.cloned.1.call-start = ((), (), s32[]{:S(2)}) async-start(), calls=%async_computation.21 | async-start | bytes 487424
  505.1 725.3 %all-reduce.23.cloned.1.call-start = ((), (), s32[]{:S(2)}) async-start(), calls=%async_computation.27 | async-start | bytes 3670016 | tf_op jit(solution)/shard_map/psum | solution.py:344
  781.2 307.9 %copy-start.29 = (f32[128,896]{1,0:T(8,128)S(1)}, f32[128,896]{1,0:T(8,128)}, u32[]{:S(2)}) copy-start(f32[128,896]{1,0:T(8,128)} %copy-done.27) | copy-start | bytes 1376260
  781.2 307.9 %copy-start.32 = (f32[128,896]{1,0:T(8,128)S(1)}, f32[128,896]{1,0:T(8,128)}, u32[]{:S(2)}) copy-start(f32[128,896]{1,0:T(8,128)} %copy-done.30) | copy-start | bytes 1376260
  (69 other events, 300.0 us)
Sparse Core Ops, SparseCore 0:
  10.2 46.5 all-gather.7
  58.9 43.5 all-gather.9
  104.7 71.8 all-gather.15
  178.5 71.9 all-gather.13
  252.5 71.9 all-gather.11
  375.4 30.0 reduce-scatter.37
  408.0 29.3 reduce-scatter.33
  439.7 29.2 reduce-scatter.35
  471.5 29.3 reduce-scatter.39
  504.2 76.9 reduce-scatter.47
  584.6 77.3 reduce-scatter.41
  665.4 113.6 reduce-scatter.49
  782.9 113.8 reduce-scatter.51
  900.1 113.9 reduce-scatter.53
  1017.5 70.9 reduce-scatter.45
  1091.5 70.5 reduce-scatter.43
  1166.1 64.2 all-reduce.22
